TPU v7x, 512 devices: a whole 4x8x8 slice. The times are simulated.
512 devices in a mesh: item: 16 (over y, core), user: 32 (over z, x).
Axes of the slice: x: 4, y: 8, z: 8, core: 2. Of those that a mesh axis runs over, the one named last changes fastest.
Arguments:
- item_factors: float32 [32768, 128], P('item')
- tile_lists: int32 [512, 16], P(('item', 'user')), may hold values from 0 to 255, as said below
- tile_weights: bfloat16 [512, 16, 128, 128], P(('item', 'user')), may hold values from 0 to 40
- user_factors: float32 [65536, 128], P(('item', 'user')), may hold values from -6 to 6
Outputs:
- new_factors: float32 [65536, 128], P(('item', 'user'))
Inputs may be any that keep to these rules, and one draw needn't show every extreme that they name: `tile_lists`: item shard s holds tiles s * 16 to (s + 1) * 16 - 1. Among the 16 slots of one device's blocks, at most 2 name tiles of one item shard, and for some shard exactly 2 do; a tile may be named more than once.
All inputs are finite; a program needn't handle non-finite values.
Results may differ from a plain program's by a relative error of at most 0.0024.
Values sent between devices are 32-bit elements; how exact they have to be, the bound alone decides.
No kernel may reach another device: no remote copies, remote signals or barrier semaphores. Data moves between devices by JAX's collectives and lax.ppermute only.
A program may use at most 64 MiB of HBM per device.

v0:
```python
import jax
import jax.numpy as jnp
from jax import lax
from jax.sharding import PartitionSpec as P

ITERS = 4
RIDGE_WEIGHT = 0.1
EPSILON = 1e-06
HIGHEST = lax.Precision.HIGHEST


def apply_system(vectors, tiles, weights, gram):
    scores = jnp.einsum("bur,bkir->bkui", vectors, tiles, precision=HIGHEST)
    spread = jnp.einsum("bkui,bkir->bur", scores * weights, tiles, precision=HIGHEST)
    return (
        spread
        + jnp.einsum("bur,rs->bus", vectors, gram, precision=HIGHEST)
        + RIDGE_WEIGHT * vectors
    )


def conjugate(start, tiles, weights, gram, steps):
    weights = weights.astype(jnp.float32)
    target = jnp.einsum("bkui,bkir->bur", 1.0 + weights, tiles, precision=HIGHEST)
    answer = start
    resid = target - apply_system(start, tiles, weights, gram)
    direction = resid
    norm_now = jnp.sum(resid * resid, axis=-1, keepdims=True)
    for step_index in range(steps):
        image = apply_system(direction, tiles, weights, gram)
        alpha = norm_now / (jnp.sum(direction * image, axis=-1, keepdims=True) + EPSILON)
        answer = answer + alpha * direction
        resid = resid - alpha * image
        norm_next = jnp.sum(resid * resid, axis=-1, keepdims=True)
        direction = resid + norm_next / (norm_now + EPSILON) * direction
        norm_now = norm_next
    return answer


def local(item_factors, tile_lists, tile_weights, user_factors):
    factor_rank = item_factors.shape[1]
    tile_side = tile_weights.shape[-1]
    blocks_here, slots_here = tile_lists.shape
    shard_rows = item_factors.shape[0]
    user_parts = lax.axis_size("user")
    share_rows = shard_rows // user_parts
    piece = lax.dynamic_slice_in_dim(
        item_factors, lax.axis_index("user") * share_rows, share_rows, 0
    )
    partial_gram = jnp.dot(piece.T, piece, precision=HIGHEST, preferred_element_type=jnp.float32)
    gram = lax.psum(partial_gram, ("item", "user"))
    tile_ids = tile_lists.reshape(-1)
    all_rows = lax.all_gather(item_factors, "item", axis=0, tiled=True)
    fetched = all_rows.reshape(-1, tile_side, factor_rank)[tile_ids]
    tiles = fetched.reshape(blocks_here, slots_here, tile_side, factor_rank)
    start = user_factors.reshape(blocks_here, tile_side, factor_rank)
    solved = conjugate(start, tiles, tile_weights, gram, ITERS)
    return solved.reshape(-1, factor_rank)


def solution(mesh):
    in_specs = (
        P("item", None),
        P(("item", "user"), None),
        P(("item", "user"), None, None, None),
        P(("item", "user"), None),
    )
    out_specs = P(("item", "user"), None)
    return jax.shard_map(local, mesh=mesh, in_specs=in_specs, out_specs=out_specs, check_vma=False)
```

profile of v0, /device:TPU:1, one launch (start us, length us, event | category | flops | bytes accessed | tf_op | source)
XLA Modules:
  0.0 362.3 jit_solution(888267724627594206)
XLA Ops:
  7.4 0.0 all-gather.2.cloned.1.call-start
  7.4 0.7 all-gather.2.cloned.1.call-update
  8.1 0.0 all-reduce.2.cloned.1.call-start
  8.1 1.8 fusion.22
  9.9 0.0 all-reduce.2.cloned.1.call-update
  9.9 0.7 fusion.24
  10.6 1.3 copy.24
  11.9 0.9 copy.33
  12.8 101.3 %all-gather.2.cloned.1.call-done = f32[32768,128]{1,0:T(8,128)} async-done(((f32[2048,128]{1,0:T(8,128)}), f32[32768,128]{1,0:T(8,128)}) %all-gather.2.cloned.1.call-update) | async-done | bytes 16777232 | tf_op jit(solution)/shard_map/all_gather | solution.py:53
  114.2 6.4 %gather_fusion = f32[16,128,128]{2,1,0:T(8,128)S(1)} fusion(f32[256,128,128]{2,1,0:T(8,128)} %bitcast.119, s32[1024]{0:T(1024)S(1)} %pad_clamp_fusion), kind=kCustom, calls=%fused_computation | custom fusion | bytes 2097216 | tf_op jit(solution)/shard_map/gather | solution.py:54
  120.6 1.8 fusion
  122.4 1.8 convolution_bitcast_fusion.10
  124.2 1.8 convolution_bitcast_fusion.11
  126.1 211.4 %all-reduce.2.cloned.1.call-done = f32[128,128]{1,0:T(8,128)} async-done(((f32[128,128]{1,0:T(8,128)}), f32[128,128]{1,0:T(8,128)}) %all-reduce.2.cloned.1.call-update) | async-done | bytes 65552 | tf_op jit(solution)/shard_map/psum | solution.py:51
  337.5 0.0 copy-start
  337.5 1.2 fusion.12
  338.7 1.0 fusion.1
  339.7 1.8 convolution_bitcast_fusion.8
  341.5 1.1 multiply_reduce_fusion.5
  342.7 1.0 fusion.2
  343.7 1.8 convolution_bitcast_fusion.7
  345.5 1.1 multiply_reduce_fusion.3
  346.8 1.2 fusion.3
  347.9 1.8 convolution_bitcast_fusion.6
  349.8 1.1 multiply_reduce_fusion.1
  351.0 1.0 fusion.4
  352.0 1.8 convolution_bitcast_fusion.5
  353.8 0.0 copy-done
  353.8 0.3 fusion.13
  354.2 0.7 copy.43
  (15 shorter events, 0.3 us)
Async XLA Ops:
  7.4 106.8 %all-gather.2.cloned.1.call-start = ((), (), s32[]{:S(2)}) async-start(), calls=%async_computation | async-start | bytes 17825792 | tf_op jit(solution)/shard_map/all_gather | solution.py:53
  8.1 329.4 %all-reduce.2.cloned.1.call-start = ((), (), s32[]{:S(2)}) async-start(), calls=%async_computation.1 | async-start | bytes 131072 | tf_op jit(solution)/shard_map/psum | solution.py:51
  337.5 16.3 %copy-start = (f32[128,128]{1,0:T(8,128)S(1)}, f32[128,128]{1,0:T(8,128)}, u32[]{:S(2)}) copy-start(f32[128,128]{1,0:T(8,128)} %all-reduce.2.cloned.1.call-done) | copy-start | bytes 196612
Sparse Core Ops, SparseCore 0:
  10.3 103.8 all-gather.1
Sparse Core Ops, SparseCore 1:
  13.6 323.9 all-reduce.1
where the time goes:
time: 363 us; the launch traced here: 362 us
  waiting for transfers between devices  313 us (86%)
  matrix products  23.5 us (6%)
  between operations  15 us (4%)
  local copies, waits for them, and re-layouts  9.38 us (3%)
    psum x1, waiting for transfers between devices, local(): gram = lax.psum(partial_gram, ('item', 'user'))  211 us
    all_gather x1, waiting for transfers between devices, local(): all_rows = lax.all_gather(item_factors, 'item', axis=0, tiled=True)  101 us
    dot_general x5, matrix products, apply_system(): jnp.einsum('bkui,bkir->bur', scores * weights, tiles, precision=HIGHEST)  9.1 us
  transfers between devices with their start and end apart: 2, of which 2 were waited for; matrix products, arithmetic and copies ran while one was open for 5% of the time, Pallas kernels for 0%

commit v1 on v0

--- a/solution.py
+++ b/solution.py
@@ -48,7 +48,7 @@
         item_factors, lax.axis_index("user") * share_rows, share_rows, 0
     )
     partial_gram = jnp.dot(piece.T, piece, precision=HIGHEST, preferred_element_type=jnp.float32)
-    gram = lax.psum(partial_gram, ("item", "user"))
+    gram = jax.lax.psum(jax.lax.psum(partial_gram, "item"), "user")
     tile_ids = tile_lists.reshape(-1)
     all_rows = lax.all_gather(item_factors, "item", axis=0, tiled=True)
     fetched = all_rows.reshape(-1, tile_side, factor_rank)[tile_ids]

time: 363 us -> 399 us (1.099)
  waiting for transfers between devices: 313 us -> 348 us
    psum x1 -> x2, waiting for transfers between devices: 211 us -> 248 us  [local(): gram = jax.lax.psum(jax.lax.psum(partial_gram, 'item'), 'user')]
  transfers between devices with their start and end apart: 2 -> 3, of which waited for: 2 -> 3; matrix products, arithmetic and copies ran while one was open for 5% -> 4% of each run, Pallas kernels for 0% -> 0%
where the time goes in v1:
time: 399 us; the launch traced here: 395 us
  waiting for transfers between devices  348 us (87%)
  matrix products  23.5 us (6%)
  between operations  13.2 us (3%)
  local copies, waits for them, and re-layouts  9.36 us (2%)
    psum x2, waiting for transfers between devices, local(): gram = jax.lax.psum(jax.lax.psum(partial_gram, 'item'), 'user')  248 us
    all_gather x1, waiting for transfers between devices, local(): all_rows = lax.all_gather(item_factors, 'item', axis=0, tiled=True)  98.7 us
    dot_general x5, matrix products, apply_system(): jnp.einsum('bkui,bkir->bur', scores * weights, tiles, precision=HIGHEST)  9.1 us
  transfers between devices with their start and end apart: 3, of which 3 were waited for; matrix products, arithmetic and copies ran while one was open for 4% of the time, Pallas kernels for 0%

profile of v1, /device:TPU:1, one launch (start us, length us, event | category | flops | bytes accessed | tf_op | source)
XLA Modules:
  0.0 395.1 jit_solution(348700483169526037)
XLA Ops:
  6.5 0.0 all-reduce.3.cloned.1.call-start
  6.5 1.8 fusion.22
  8.3 0.0 all-reduce.3.cloned.1.call-update
  8.3 0.0 all-gather.2.cloned.1.call-start
  8.4 0.7 all-gather.2.cloned.1.call-update
  9.1 0.0 all-reduce.5.cloned.1.call-start
  9.1 1.3 copy.24
  10.4 0.9 copy.33
  11.4 0.7 fusion.24
  12.0 109.6 %all-reduce.3.cloned.1.call-done = f32[128,128]{1,0:T(8,128)} async-done(((f32[128,128]{1,0:T(8,128)}), f32[128,128]{1,0:T(8,128)}) %all-reduce.3.cloned.1.call-update) | async-done | bytes 65552 | tf_op jit(solution)/shard_map/psum | solution.py:51
  121.6 0.0 all-reduce.5.cloned.1.call-update
  121.6 98.7 %all-gather.2.cloned.1.call-done = f32[32768,128]{1,0:T(8,128)} async-done(((f32[2048,128]{1,0:T(8,128)}), f32[32768,128]{1,0:T(8,128)}) %all-gather.2.cloned.1.call-update) | async-done | bytes 16777232 | tf_op jit(solution)/shard_map/all_gather | solution.py:53
  220.4 6.4 %gather_fusion = f32[16,128,128]{2,1,0:T(8,128)S(1)} fusion(f32[256,128,128]{2,1,0:T(8,128)} %bitcast.119, s32[1024]{0:T(1024)S(1)} %pad_clamp_fusion), kind=kCustom, calls=%fused_computation | custom fusion | bytes 2097216 | tf_op jit(solution)/shard_map/gather | solution.py:54
  226.8 1.8 fusion
  228.6 1.8 convolution_bitcast_fusion.10
  230.4 1.8 convolution_bitcast_fusion.11
  232.2 138.9 %all-reduce.5.cloned.1.call-done = f32[128,128]{1,0:T(8,128)} async-done(((f32[128,128]{1,0:T(8,128)}), f32[128,128]{1,0:T(8,128)}) %all-reduce.5.cloned.1.call-update) | async-done | bytes 65552 | tf_op jit(solution)/shard_map/psum | solution.py:51
  371.1 0.0 copy-start
  371.1 1.2 fusion.12
  372.3 1.0 fusion.1
  373.3 1.8 convolution_bitcast_fusion.8
  375.1 1.1 multiply_reduce_fusion.5
  376.4 1.0 fusion.2
  377.3 1.8 convolution_bitcast_fusion.7
  379.1 1.1 multiply_reduce_fusion.3
  380.4 1.2 fusion.3
  381.6 1.8 convolution_bitcast_fusion.6
  383.4 1.1 multiply_reduce_fusion.1
  384.6 1.0 fusion.4
  385.6 1.8 convolution_bitcast_fusion.5
  387.4 0.0 copy-done
  387.4 0.3 fusion.13
  387.8 0.7 copy.43
  (15 shorter events, 0.3 us)
Async XLA Ops:
  6.5 115.1 %all-reduce.3.cloned.1.call-start = ((), (), s32[]{:S(2)}) async-start(), calls=%async_computation.1 | async-start | bytes 131072 | tf_op jit(solution)/shard_map/psum | solution.py:51
  8.3 212.1 %all-gather.2.cloned.1.call-start = ((), (), s32[]{:S(2)}) async-start(), calls=%async_computation | async-start | bytes 17825792 | tf_op jit(solution)/shard_map/all_gather | solution.py:53
  9.1 362.0 %all-reduce.5.cloned.1.call-start = ((), (), s32[]{:S(2)}) async-start(), calls=%async_computation.2 | async-start | bytes 131072 | tf_op jit(solution)/shard_map/psum | solution.py:51
  371.1 16.3 %copy-start = (f32[128,128]{1,0:T(8,128)S(1)}, f32[128,128]{1,0:T(8,128)}, u32[]{:S(2)}) copy-start(f32[128,128]{1,0:T(8,128)} %all-reduce.5.cloned.1.call-done) | copy-start | bytes 196612
Sparse Core Ops, SparseCore 0:
  9.7 111.9 all-reduce.2
  123.7 96.6 all-gather.1
  223.8 147.2 all-reduce.4
